TPU v7x, 32 devices: a whole 2x2x4 slice. The times are simulated.
32 devices in a mesh: rows: 4 (over x, core), cols: 8 (over z, y).
Axes of the slice: x: 2, y: 2, z: 4, core: 2. Of those that a mesh axis runs over, the one named last changes fastest.
Arguments:
- pair_integrals: float32 [4096, 4096], P('rows', 'cols'), may hold values from -6 to 6
- left_factor: float32 [4096, 1024], P('rows', 'cols'), may hold values from -0.9375 to 0.9375
- core: float32 [1024, 1024], replicated, may hold values from -6 to 6
- right_factor: float32 [4096, 1024], P('cols', 'rows'), may hold values from -0.9375 to 0.9375
Outputs:
- core_next: float32 [1024, 1024], replicated
All inputs are finite; a program needn't handle non-finite values.
Results may differ from a plain program's by a relative error of at most 0.000062.
Values sent between devices are 32-bit elements; how exact they have to be, the bound alone decides.
No kernel may reach another device: no remote copies, remote signals or barrier semaphores. Data moves between devices by JAX's collectives and lax.ppermute only.
A program may use at most 128 MiB of HBM per device.

v0:
```python
import jax
import jax.numpy as jnp
from jax import lax
from jax.sharding import PartitionSpec as P


def product(left, right):
    return jnp.dot(left, right, precision=lax.Precision.HIGHEST, preferred_element_type=jnp.float32)


def shards(pair_integrals, left_factor, core, right_factor):
    left_rows = lax.all_gather(left_factor, "cols", axis=1, tiled=True)
    right_rows = lax.all_gather(right_factor, "rows", axis=1, tiled=True)
    mixed = product(core, right_rows.T)
    residual = pair_integrals - product(left_rows, mixed)
    along = product(residual, right_rows)
    local_term = product(left_rows.T, along)
    gradient = lax.psum(local_term, ("rows", "cols"))
    numer = jnp.sum(gradient * gradient)
    image = product(left_rows, product(gradient, right_rows.T))
    denom = lax.psum(jnp.sum(image * image), ("rows", "cols"))
    return core + numer / denom * gradient


def solution(mesh):
    return jax.shard_map(
        shards,
        mesh=mesh,
        in_specs=(P("rows", "cols"), P("rows", "cols"), P(), P("cols", "rows")),
        out_specs=P(),
        check_vma=False,
    )
```

profile of v0, /device:TPU:0, one launch (start us, length us, event | category | flops | bytes accessed | tf_op | source)
XLA Modules:
  0.0 382.8 jit_solution(6131846957028007544)
XLA Ops:
  6.5 0.0 all-gather.3.cloned.1.call-start
  6.5 0.7 all-gather.3.cloned.1.call-update
  7.3 0.0 all-gather.5.cloned.1.call-start
  7.3 0.7 all-gather.5.cloned.1.call-update
  8.0 0.0 all-reduce.2.cloned.1.call-start
  8.1 26.2 %all-gather.3.cloned.1.call-done = f32[512,1024]{1,0:T(8,128)} async-done(((f32[512,256]{1,0:T(8,128)}), f32[512,1024]{1,0:T(8,128)}) %all-gather.3.cloned.1.call-update) | async-done | bytes 2097168 | tf_op jit(solution)/shard_map/all_gather | solution.py:13
  34.2 10.2 %fusion.1 = f32[1024,512]{1,0:T(8,128)} fusion(f32[1024,1024]{1,0:T(8,128)} %param.6, f32[512,1024]{1,0:T(8,128)} %all-gather.3.cloned.1.call-done), kind=kOutput, calls=%fused_computation.6 | convolution fusion | flops 6442450944 | bytes 8388608 | tf_op jit(solution)/shard_map/dot_general | solution.py:8
  44.5 66.5 %all-gather.5.cloned.1.call-done = f32[1024,1024]{1,0:T(8,128)} async-done(((f32[1024,128]{1,0:T(8,128)}), f32[1024,1024]{1,0:T(8,128)}) %all-gather.5.cloned.1.call-update) | async-done | bytes 4194320 | tf_op jit(solution)/shard_map/all_gather | solution.py:12
  110.9 10.0 %fusion.2 = f32[512,1024]{0,1:T(8,128)S(1)} fusion(f32[1024,512]{1,0:T(8,128)} %fusion.1, f32[1024,1024]{1,0:T(8,128)} %all-gather.5.cloned.1.call-done), kind=kOutput, calls=%fused_computation.7 | convolution fusion | flops 6442450944 | bytes 8388608 | tf_op jit(solution)/shard_map/dot_general | solution.py:8
  120.9 0.0 copy-done
  120.9 0.0 copy-done.3
  120.9 0.0 copy-start.1
  120.9 6.9 %fusion = f32[1024,1024]{1,0:T(8,128)S(1)} fusion(f32[512,1024]{1,0:T(8,128)S(1)} %copy-done, f32[1024,512]{1,0:T(8,128)S(1)} %copy-done.3, f32[512,1024]{0,1:T(8,128)S(1)} %fusion.2), kind=kOutput, calls=%fused_computation.4 | convolution fusion | flops 6442975232 | bytes 10485760 | tf_op jit(solution)/shard_map/dot_general | solution.py:8
  127.8 0.0 copy-done.1
  127.8 14.9 %convolution_bitcast_fusion = f32[1024,1024]{0,1:T(8,128)} fusion(f32[1024,1024]{1,0:T(8,128)S(1)} %fusion, f32[1024,1024]{1,0:T(8,128)S(1)} %copy-done.1), kind=kOutput, calls=%fused_computation.2 | convolution fusion | flops 12884901888 | bytes 12582912 | tf_op jit(solution)/shard_map/dot_general | solution.py:8
  142.7 0.0 all-reduce.2.cloned.1.call-update
  142.7 140.8 %all-reduce.2.cloned.1.call-done = f32[1024,1024]{0,1:T(8,128)} async-done(((f32[1024,1024]{0,1:T(8,128)}), f32[1024,1024]{0,1:T(8,128)}) %all-reduce.2.cloned.1.call-update) | async-done | bytes 4194320 | tf_op jit(solution)/shard_map/psum | solution.py:18
  283.5 15.6 %fusion.3 = f32[1024,512]{1,0:T(8,128)S(1)} fusion(f32[1024,1024]{0,1:T(8,128)} %all-reduce.2.cloned.1.call-done, f32[512,1024]{1,0:T(8,128)S(1)} %copy-done), kind=kOutput, calls=%fused_computation.8 | convolution fusion | flops 6442450944 | bytes 8388608 | tf_op jit(solution)/shard_map/dot_general | solution.py:8
  299.2 14.3 %multiply_reduce_fusion.1 = f32[]{:T(128)} fusion(f32[1024,512]{1,0:T(8,128)S(1)} %fusion.3, f32[1024,1024]{1,0:T(8,128)S(1)} %copy-done.2), kind=kOutput, calls=%fused_computation.5 | convolution fusion | flops 6443499520 | bytes 6291460 | tf_op jit(solution)/shard_map/dot_general | solution.py:8
  313.5 5.3 %copy.5 = f32[1024,1024]{0,1:T(8,128)} copy(f32[1024,1024]{1,0:T(8,128)} %param.6) | data formatting | bytes 8388608 | tf_op args[2]
  318.9 39.5 %psum.15 = f32[]{:T(128)} all-reduce(f32[]{:T(128)} %multiply_reduce_fusion.1), channel_id=1, replica_groups=mesh['rows'=4,'cols'=8] {'rows','cols'}, use_global_device_ids=true, to_apply=%region_3.0 | all-reduce | flops 1 | bytes 8 | tf_op jit(solution)/shard_map/psum | solution.py:21
  358.3 3.9 %multiply_reduce_fusion = f32[]{:T(128)} fusion(f32[1024,1024]{0,1:T(8,128)} %all-reduce.2.cloned.1.call-done), kind=kLoop, calls=%fused_computation.1 | loop fusion | flops 2097151 | bytes 4194308 | tf_op jit(solution)/shard_map/reduce_sum | solution.py:19
  363.6 6.9 %multiply_add_fusion = f32[1024,1024]{0,1:T(8,128)} fusion(f32[1024,1024]{0,1:T(8,128)} %copy.5, f32[1024,1024]{0,1:T(8,128)} %all-reduce.2.cloned.1.call-done, f32[]{:T(128)S(6)} %div.3), kind=kLoop, calls=%fused_computation | loop fusion | flops 2097152 | bytes 12582916 | tf_op jit(solution)/shard_map/add | solution.py:22
  370.4 5.3 %copy.6 = f32[1024,1024]{1,0:T(8,128)} copy(f32[1024,1024]{0,1:T(8,128)} %multiply_add_fusion) | data formatting | bytes 8388608 | tf_op jit(solution)/shard_map/add | solution.py:22
  (4 shorter events, 0.0 us)
Async XLA Ops:
  6.5 27.7 %all-gather.3.cloned.1.call-start = ((), (), s32[]{:S(2)}) async-start(), calls=%async_computation | async-start | bytes 2621440 | tf_op jit(solution)/shard_map/all_gather | solution.py:13
  7.3 103.7 %all-gather.5.cloned.1.call-start = ((), (), s32[]{:S(2)}) async-start(), calls=%async_computation.1 | async-start | bytes 4718592 | tf_op jit(solution)/shard_map/all_gather | solution.py:12
  8.0 275.5 %all-reduce.2.cloned.1.call-start = ((), (), s32[]{:S(2)}) async-start(), calls=%async_computation.2 | async-start | bytes 8388608 | tf_op jit(solution)/shard_map/psum | solution.py:18
  44.5 76.4 %copy-start = (f32[512,1024]{1,0:T(8,128)S(1)}, f32[512,1024]{1,0:T(8,128)}, u32[]{:S(2)}) copy-start(f32[512,1024]{1,0:T(8,128)} %all-gather.3.cloned.1.call-done) | copy-start | bytes 6291460
  110.9 10.0 %copy-start.3 = (f32[1024,512]{1,0:T(8,128)S(1)}, f32[1024,512]{1,0:T(8,128)}, u32[]{:S(2)}) copy-start(f32[1024,512]{1,0:T(8,128)} %param.4) | copy-start | bytes 6291460
  120.9 6.9 %copy-start.1 = (f32[1024,1024]{1,0:T(8,128)S(1)}, f32[1024,1024]{1,0:T(8,128)}, u32[]{:S(2)}) copy-start(f32[1024,1024]{1,0:T(8,128)} %all-gather.5.cloned.1.call-done) | copy-start | bytes 12582916
  283.5 15.6 %copy-start.2 = (f32[1024,1024]{1,0:T(8,128)S(1)}, f32[1024,1024]{1,0:T(8,128)}, u32[]{:S(2)}) copy-start(f32[1024,1024]{1,0:T(8,128)} %all-gather.5.cloned.1.call-done) | copy-start | bytes 12582916
Sparse Core Ops, SparseCore 0:
  8.9 25.2 all-gather.2
  36.2 74.6 all-gather.4
  142.9 140.6 all-reduce.1
where the time goes:
time: 389 us; the launch traced here: 383 us
  waiting for transfers between devices  235 us (60%)
  matrix products  72 us (19%)
  blocking collectives  39.5 us (10%)
  between operations  15 us (4%)
  other arithmetic  10.8 us (3%)
  local copies, waits for them, and re-layouts  10.7 us (3%)
    psum x1, waiting for transfers between devices, shards(): gradient = lax.psum(local_term, ('rows', 'cols'))  141 us
    dot_general x6, matrix products, product(): jnp.dot(left, right, precision=lax.Precision.HIGHEST, preferred_element_t...  72 us
    all_gather x1, waiting for transfers between devices, shards(): left_rows = lax.all_gather(left_factor, 'cols', axis=1, tiled=True)  66.5 us
    psum x1, blocking collectives, shards(): denom = lax.psum(jnp.sum(image * image), ('rows', 'cols'))  39.5 us
    all_gather x1, waiting for transfers between devices, shards(): right_rows = lax.all_gather(right_factor, 'rows', axis=1, tiled=True)  26.2 us
  transfers between devices with their start and end apart: 3, of which 3 were waited for; matrix products, arithmetic and copies ran while one was open for 3% of the time, Pallas kernels for 0%

commit v1 on v0

--- a/solution.py
+++ b/solution.py
@@ -1,7 +1,24 @@
+import functools
 import jax
 import jax.numpy as jnp
 from jax import lax
 from jax.sharding import PartitionSpec as P
+
+
+def process_shifts_all_for(work_x, row_axis):
+    axis_len = lax.psum(1, row_axis)
+    v_next = sorted(((p, (p + 1) % axis_len) for p in range(axis_len)))
+    local_now = work_x
+    block_list = [local_now]
+    for t in range(1, axis_len):
+        local_now = lax.ppermute(local_now, row_axis, v_next)
+        block_list.insert(0, local_now)
+    x_next = jnp.concatenate(block_list, 1)
+    f_next = lax.axis_index(row_axis) + 1
+    return jnp.roll(x_next, shift=f_next * work_x.shape[1], axis=1)
+
+
+panel_handle = functools.partial(process_shifts_all_for, row_axis="rows")
 
 
 def product(left, right):
@@ -10,7 +27,7 @@
 
 def shards(pair_integrals, left_factor, core, right_factor):
     left_rows = lax.all_gather(left_factor, "cols", axis=1, tiled=True)
-    right_rows = lax.all_gather(right_factor, "rows", axis=1, tiled=True)
+    right_rows = panel_handle(right_factor)
     mixed = product(core, right_rows.T)
     residual = pair_integrals - product(left_rows, mixed)
     along = product(residual, right_rows)

time: 389 us -> 365 us (0.938)
  waiting for transfers between devices: 235 us -> 210 us
    ppermute x0 -> x3, waiting for transfers between devices: none -> 26.2 us  [process_shifts_all_for(): local_now = lax.ppermute(local_now, row_axis, v_next)]
    all_gather x1 -> x0, waiting for transfers between devices: 26.2 us -> none  [shards(): right_rows = lax.all_gather(right_factor, 'rows', axis=1, tiled=True)]
    all_gather x1, waiting for transfers between devices: 66.5 us -> 42.1 us  [shards(): left_rows = lax.all_gather(left_factor, 'cols', axis=1, tiled=True)]
    unnamed x9 -> x22, local copies, waits for them, and re-layouts: 5.35 us -> 8.9 us
  transfers between devices with their start and end apart: 3 -> 5, of which waited for: 3 -> 5; matrix products, arithmetic and copies ran while one was open for 3% -> 2% of each run, Pallas kernels for 0% -> 0%
where the time goes in v1:
time: 365 us; the launch traced here: 359 us
  waiting for transfers between devices  210 us (58%)
  matrix products  68.6 us (19%)
  blocking collectives  39.5 us (11%)
  between operations  15.3 us (4%)
  local copies, waits for them, and re-layouts  14.3 us (4%)
  other arithmetic  10.8 us (3%)
    psum x1, waiting for transfers between devices, shards(): gradient = lax.psum(local_term, ('rows', 'cols'))  141 us
    dot_general x6, matrix products, product(): jnp.dot(left, right, precision=lax.Precision.HIGHEST, preferred_element_t...  68.6 us
    all_gather x1, waiting for transfers between devices, shards(): left_rows = lax.all_gather(left_factor, 'cols', axis=1, tiled=True)  42.1 us
    psum x1, blocking collectives, shards(): denom = lax.psum(jnp.sum(image * image), ('rows', 'cols'))  39.5 us
    ppermute x3, waiting for transfers between devices, process_shifts_all_for(): local_now = lax.ppermute(local_now, row_axis, v_next)  26.2 us
    unnamed x22, local copies, waits for them, and re-layouts  8.9 us
  transfers between devices with their start and end apart: 5, of which 5 were waited for; matrix products, arithmetic and copies ran while one was open for 2% of the time, Pallas kernels for 0%

profile of v1, /device:TPU:0, one launch (start us, length us, event | category | flops | bytes accessed | tf_op | source)
XLA Modules:
  0.0 359.0 jit_solution(8558803927966363968)
XLA Ops:
  6.5 0.7 all-gather.2.cloned.1.call-update
  7.3 0.5 collective-permute-start
  7.8 9.0 %collective-permute-done = f32[512,256]{1,0:T(8,128)S(1)} collective-permute-done((f32[512,256]{1,0:T(8,128)}, f32[512,256]{1,0:T(8,128)S(1)}, u32[]{:S(2)}, u32[]{:S(2)}) %collective-permute-start) | collective-permute-done | bytes 524320 | tf_op jit(solution)/shard_map/ppermute | solution.py:14
  16.9 8.6 %collective-permute-done.1 = f32[512,256]{1,0:T(8,128)S(1)} collective-permute-done((f32[512,256]{1,0:T(8,128)S(1)}, f32[512,256]{1,0:T(8,128)S(1)}, u32[]{:S(2)}, u32[]{:S(2)}) %collective-permute-start.1) | collective-permute-done | bytes 524320 | tf_op jit(solution)/shard_map/ppermute | solution.py:14
  25.5 8.6 %collective-permute-done.2 = f32[512,256]{1,0:T(8,128)S(1)} collective-permute-done((f32[512,256]{1,0:T(8,128)S(1)}, f32[512,256]{1,0:T(8,128)S(1)}, u32[]{:S(2)}, u32[]{:S(2)}) %collective-permute-start.2) | collective-permute-done | bytes 524320 | tf_op jit(solution)/shard_map/ppermute | solution.py:14
  34.1 0.1 constant_dynamic-update-slice_fusion.6
  34.2 0.1 constant_dynamic-update-slice_fusion.5
  34.3 1.1 constant_dynamic-update-slice_fusion.4
  35.5 0.1 constant_dynamic-update-slice_fusion.2
  35.6 0.1 constant_dynamic-update-slice_fusion.1
  35.7 2.0 copy-done.1
  37.7 7.0 %fusion.4 = f32[512,1024]{1,0:T(8,128)S(1)} fusion(f32[1024,1024]{1,0:T(8,128)S(1)} %copy-done, f32[512,2048]{1,0:T(8,128)S(1)} %constant_dynamic-update-slice_fusion, s32[]{:T(128)S(6)} %select_n.14), kind=kOutput, calls=%fused_computation.9 | convolution fusion | flops 6442450944 | bytes 8388612 | tf_op jit(solution)/shard_map/dot_general | solution.py:25
  44.7 42.1 %all-gather.2.cloned.1.call-done = f32[1024,1024]{1,0:T(8,128)} async-done(((f32[1024,128]{1,0:T(8,128)}), f32[1024,1024]{1,0:T(8,128)}) %all-gather.2.cloned.1.call-update) | async-done | bytes 4194320 | tf_op jit(solution)/shard_map/all_gather | solution.py:29
  86.8 9.4 %fusion.9 = f32[512,1024]{0,1:T(8,128)S(1)} fusion(f32[512,1024]{1,0:T(8,128)S(1)} %fusion.4, f32[1024,1024]{1,0:T(8,128)} %all-gather.2.cloned.1.call-done), kind=kOutput, calls=%fused_computation.22 | convolution fusion | flops 6442450944 | bytes 8388608 | tf_op jit(solution)/shard_map/dot_general | solution.py:25
  96.2 6.9 %fusion = f32[1024,1024]{1,0:T(8,128)S(1)} fusion(f32[1024,512]{1,0:T(8,128)S(1)} %copy-done.3, f32[512,1024]{0,1:T(8,128)S(1)} %fusion.9, f32[512,2048]{1,0:T(8,128)S(1)} %copy-done.2, s32[]{:T(128)S(6)} %select_n.14), kind=kOutput, calls=%fused_computation.4 | convolution fusion | flops 6442975232 | bytes 10485764 | tf_op jit(solution)/shard_map/dot_general | solution.py:25
  103.1 15.0 %convolution_bitcast_fusion = f32[1024,1024]{0,1:T(8,128)} fusion(f32[1024,1024]{1,0:T(8,128)S(1)} %fusion, f32[1024,1024]{1,0:T(8,128)S(1)} %copy-done.4), kind=kOutput, calls=%fused_computation.2 | convolution fusion | flops 12884901888 | bytes 12582912 | tf_op jit(solution)/shard_map/dot_general | solution.py:25
  118.1 140.9 %all-reduce.2.cloned.1.call-done = f32[1024,1024]{0,1:T(8,128)} async-done(((f32[1024,1024]{0,1:T(8,128)}), f32[1024,1024]{0,1:T(8,128)}) %all-reduce.2.cloned.1.call-update) | async-done | bytes 4194320 | tf_op jit(solution)/shard_map/psum | solution.py:35
  259.0 16.0 %fusion.1 = f32[1024,512]{1,0:T(8,128)S(1)} fusion(f32[1024,1024]{0,1:T(8,128)} %all-reduce.2.cloned.1.call-done, f32[512,2048]{1,0:T(8,128)} %copy-done.1, s32[]{:T(128)S(6)} %select_n.14), kind=kOutput, calls=%fused_computation.6 | convolution fusion | flops 6442450944 | bytes 8388612 | tf_op jit(solution)/shard_map/dot_general | solution.py:25
  275.1 14.3 %multiply_reduce_fusion.1 = f32[]{:T(128)} fusion(f32[1024,512]{1,0:T(8,128)S(1)} %fusion.1, f32[1024,1024]{1,0:T(8,128)S(1)} %copy-done.5), kind=kOutput, calls=%fused_computation.5 | convolution fusion | flops 6443499520 | bytes 6291460 | tf_op jit(solution)/shard_map/dot_general | solution.py:25
  289.4 5.3 %copy.5 = f32[1024,1024]{0,1:T(8,128)} copy(f32[1024,1024]{1,0:T(8,128)} %param.6) | data formatting | bytes 8388608 | tf_op args[2]
  294.7 39.5 %psum.15 = f32[]{:T(128)} all-reduce(f32[]{:T(128)} %multiply_reduce_fusion.1), channel_id=1, replica_groups=mesh['rows'=4,'cols'=8] {'rows','cols'}, use_global_device_ids=true, to_apply=%region_3.4 | all-reduce | flops 1 | bytes 8 | tf_op jit(solution)/shard_map/psum | solution.py:38
  334.2 3.9 %multiply_reduce_fusion = f32[]{:T(128)} fusion(f32[1024,1024]{0,1:T(8,128)} %all-reduce.2.cloned.1.call-done), kind=kLoop, calls=%fused_computation.1 | loop fusion | flops 2097151 | bytes 4194308 | tf_op jit(solution)/shard_map/reduce_sum | solution.py:36
  339.5 6.9 %multiply_add_fusion = f32[1024,1024]{0,1:T(8,128)} fusion(f32[1024,1024]{0,1:T(8,128)} %copy.5, f32[1024,1024]{0,1:T(8,128)} %all-reduce.2.cloned.1.call-done, f32[]{:T(128)S(6)} %div.3), kind=kLoop, calls=%fused_computation | loop fusion | flops 2097152 | bytes 12582916 | tf_op jit(solution)/shard_map/add | solution.py:39
  346.4 5.3 %copy.6 = f32[1024,1024]{1,0:T(8,128)} copy(f32[1024,1024]{0,1:T(8,128)} %multiply_add_fusion) | data formatting | bytes 8388608 | tf_op jit(solution)/shard_map/add | solution.py:39
  (21 shorter events, 0.3 us)
Async XLA Ops:
  6.5 29.1 %copy-start.6 = (f32[512,256]{1,0:T(8,128)S(1)}, f32[512,256]{1,0:T(8,128)}, u32[]{:S(2)}) copy-start(f32[512,256]{1,0:T(8,128)} %param.7) | copy-start | bytes 1572868
  6.5 80.2 %all-gather.2.cloned.1.call-start = ((), (), s32[]{:S(2)}) async-start(), calls=%async_computation | async-start | bytes 4718592 | tf_op jit(solution)/shard_map/all_gather | solution.py:29
  7.3 251.7 %all-reduce.2.cloned.1.call-start = ((), (), s32[]{:S(2)}) async-start(), calls=%async_computation.1 | async-start | bytes 8388608 | tf_op jit(solution)/shard_map/psum | solution.py:35
  7.3 9.5 %collective-permute-start = (f32[512,256]{1,0:T(8,128)}, f32[512,256]{1,0:T(8,128)S(1)}, u32[]{:S(2)}, u32[]{:S(2)}) collective-permute-start(f32[512,256]{1,0:T(8,128)} %param.7), channel_id=1, source_target_pairs={{0,8},{8,16},{16,24},{24,0},{1,9},{9,17},{17,25},{25,1},{2,10},{10... | collective-permute-start | bytes 1572872 | tf_op jit(solution)/shard_map/ppermute | solution.py:14
  16.8 8.6 %collective-permute-start.1 = (f32[512,256]{1,0:T(8,128)S(1)}, f32[512,256]{1,0:T(8,128)S(1)}, u32[]{:S(2)}, u32[]{:S(2)}) collective-permute-start(f32[512,256]{1,0:T(8,128)S(1)} %collective-permute-done), channel_id=1, source_target_pairs={{0,8},{8,16},{16,24},{24,0},{1,9},{9,17},{17,25},{25,1},{2,10},{10... | collective-permute-start | bytes 1572872 | tf_op jit(solution)/shard_map/ppermute | solution.py:14
  25.4 8.6 %collective-permute-start.2 = (f32[512,256]{1,0:T(8,128)S(1)}, f32[512,256]{1,0:T(8,128)S(1)}, u32[]{:S(2)}, u32[]{:S(2)}) collective-permute-start(f32[512,256]{1,0:T(8,128)S(1)} %collective-permute-done.1), channel_id=1, source_target_pairs={{0,8},{8,16},{16,24},{24,0},{1,9},{9,17},{17,25},{25,1},{2,10},{10... | collective-permute-start | bytes 1572872 | tf_op jit(solution)/shard_map/ppermute | solution.py:14
  25.5 12.3 %copy-start = (f32[1024,1024]{1,0:T(8,128)S(1)}, f32[1024,1024]{1,0:T(8,128)}, u32[]{:S(2)}) copy-start(f32[1024,1024]{1,0:T(8,128)} %param.6) | copy-start | bytes 12582916
  35.7 2.0 copy-start.1
  86.8 9.4 %copy-start.2 = (f32[512,2048]{1,0:T(8,128)S(1)}, f32[512,2048]{1,0:T(8,128)}, u32[]{:S(2)}) copy-start(f32[512,2048]{1,0:T(8,128)} %copy-done.1) | copy-start | bytes 12582916
  86.8 9.4 %copy-start.3 = (f32[1024,512]{1,0:T(8,128)S(1)}, f32[1024,512]{1,0:T(8,128)}, u32[]{:S(2)}) copy-start(f32[1024,512]{1,0:T(8,128)} %param.4) | copy-start | bytes 6291460
  96.2 6.9 %copy-start.4 = (f32[1024,1024]{1,0:T(8,128)S(1)}, f32[1024,1024]{1,0:T(8,128)}, u32[]{:S(2)}) copy-start(f32[1024,1024]{1,0:T(8,128)} %all-gather.2.cloned.1.call-done) | copy-start | bytes 12582916
  259.0 16.0 %copy-start.5 = (f32[1024,1024]{1,0:T(8,128)S(1)}, f32[1024,1024]{1,0:T(8,128)}, u32[]{:S(2)}) copy-start(f32[1024,1024]{1,0:T(8,128)} %all-gather.2.cloned.1.call-done) | copy-start | bytes 12582916
Sparse Core Ops, SparseCore 0:
  9.4 77.3 all-gather.1
  118.3 140.6 all-reduce.1
